TPU v7x, 32 devices: a whole 2x2x4 slice. The times are simulated.
32 devices in a mesh: gx: 8 (over y, x, core), gy: 4 (over z).
Axes of the slice: x: 2, y: 2, z: 4, core: 2. Of those that a mesh axis runs over, the one named last changes fastest.
Arguments:
- adjoint_source: float32 [4, 64, 256, 512], P(None, 'gx', 'gy'), may hold values from -40 to 40, as said below
- conductivity: float32 [64, 256, 512], P('gx', 'gy'), may hold values from 0.1 to 10
- electrodes: int32 [4], replicated, may hold values from 0 to 16383
Outputs:
- solution_field: float32 [4, 64, 256, 512], P(None, 'gx', 'gy')
- residual: float32 [4, 64, 256, 512], P(None, 'gx', 'gy')
Inputs may be any that keep to these rules, and one draw needn't show every extreme that they name: `electrodes`: each entry is a surface cell index, its first coordinate times 256 plus its second. `adjoint_source`: drawn afresh cell by cell.
All inputs are finite; a program needn't handle non-finite values.
Results may differ from a plain program's by a relative error of at most 0.0003.
Values sent between devices are 32-bit elements; how exact they have to be, the bound alone decides.
A program may use at most 128 MiB of HBM per device.

v0:
```python
import math
import jax
import jax.numpy as jnp
from jax import lax
from jax.sharding import PartitionSpec as P

ITERS = 2


def with_halo(block, sides, width):
    for axis, dim in sides:
        count = lax.axis_size(axis)
        forward = [(i, i + 1) for i in range(count - 1)]
        backward = [(target, source) for source, target in forward]
        low = lax.ppermute(
            lax.slice_in_dim(block, block.shape[dim] - width, None, axis=dim), axis, forward
        )
        high = lax.ppermute(lax.slice_in_dim(block, 0, width, axis=dim), axis, backward)
        block = jnp.concatenate([low, block, high], axis=dim)
    return block


def face_coefficients(padded):
    center = padded[1:-1, 1:-1, 1:-1]

    def face(neighbour):
        return jnp.where(neighbour > 0.0, 0.5 * (center + neighbour), center)

    return (
        face(padded[2:, 1:-1, 1:-1]),
        face(padded[:-2, 1:-1, 1:-1]),
        face(padded[1:-1, 2:, 1:-1]),
        face(padded[1:-1, :-2, 1:-1]),
        face(padded[1:-1, 1:-1, 2:]),
        face(padded[1:-1, 1:-1, :-2]),
    )


def apply_operator(rimmed, coeffs):
    padded = jnp.pad(rimmed, ((0, 0), (0, 0), (0, 0), (1, 1)))
    center = padded[:, 1:-1, 1:-1, 1:-1]
    others = (
        padded[:, 2:, 1:-1, 1:-1],
        padded[:, :-2, 1:-1, 1:-1],
        padded[:, 1:-1, 2:, 1:-1],
        padded[:, 1:-1, :-2, 1:-1],
        padded[:, 1:-1, 1:-1, 2:],
        padded[:, 1:-1, 1:-1, :-2],
    )
    total = jnp.zeros(center.shape, jnp.float32)
    for coeff, other in zip(coeffs, others):
        total = total + coeff[None] * (center - other)
    return total


def gram(left, right):
    return jnp.einsum("ixyz,jxyz->ij", left, right, precision=lax.Precision.HIGHEST)


def combine(matrix, block):
    return jnp.einsum("ij,ixyz->jxyz", matrix, block, precision=lax.Precision.HIGHEST)


def small_solve(spd, rhs):
    factor = jnp.linalg.cholesky(spd)
    return jax.scipy.linalg.cho_solve((factor, True), rhs)


def residual_image(residual, coeffs):
    rimmed = with_halo(residual, (("gx", 1), ("gy", 2)), 1)
    return apply_operator(rimmed, coeffs)


def paired_products(residual, image):
    return lax.psum((gram(residual, residual), gram(residual, image)), ("gx", "gy"))


def shards(adjoint_source, conductivity, electrodes):
    rim_sigma = with_halo(conductivity, (("gx", 0), ("gy", 1)), 1)
    coeffs = face_coefficients(jnp.pad(rim_sigma, ((0, 0), (0, 0), (1, 1))))
    cells_x = adjoint_source.shape[1]
    cells_y = adjoint_source.shape[2]
    cells_z = adjoint_source.shape[3]
    total_x = cells_x * lax.axis_size("gx")
    total_y = cells_y * lax.axis_size("gy")
    current = math.sqrt(total_x * total_y * cells_z)
    start_x = lax.axis_index("gx") * cells_x
    start_y = lax.axis_index("gy") * cells_y
    row_x = electrodes // total_y
    row_y = electrodes % total_y
    mark_x = ((start_x + jnp.arange(cells_x, dtype=jnp.int32))[None, :] == row_x[:, None]).astype(
        jnp.float32
    )
    mark_y = ((start_y + jnp.arange(cells_y, dtype=jnp.int32))[None, :] == row_y[:, None]).astype(
        jnp.float32
    )
    spike = current * (mark_x[:, :, None] * mark_y[:, None, :])
    right_side = adjoint_source.at[:, :, :, 0].add(spike)
    solution_field = jnp.zeros_like(right_side)
    residual = right_side
    direction = right_side
    image = residual_image(residual, coeffs)
    norm_now, curvature = paired_products(residual, image)
    along = image
    for step in range(ITERS):
        alpha = small_solve(curvature, norm_now)
        solution_field = solution_field + combine(alpha, direction)
        residual = residual - combine(alpha, along)
        if step + 1 < ITERS:
            image = residual_image(residual, coeffs)
            norm_next, cross = paired_products(residual, image)
            beta = small_solve(norm_now, norm_next)
            weighted = jnp.dot(curvature, beta, precision=lax.Precision.HIGHEST)
            curvature = cross - jnp.dot(beta.T, weighted, precision=lax.Precision.HIGHEST)
            direction = residual + combine(beta, direction)
            along = image + combine(beta, along)
            norm_now = norm_next
    return (solution_field, residual)


def solution(mesh):
    placed = (P(None, "gx", "gy", None), P("gx", "gy", None), P())
    return jax.shard_map(
        shards,
        mesh=mesh,
        in_specs=placed,
        out_specs=(P(None, "gx", "gy", None), P(None, "gx", "gy", None)),
        check_vma=False,
    )
```

profile of v0, /device:TPU:0, one launch (start us, length us, event | category | flops | bytes accessed | tf_op | source)
XLA Modules:
  0.0 340.7 jit_solution(11760287476002612887)
XLA Ops:
  0.6 1.0 fusion.70
  1.6 2.4 collective-permute-start.2
  4.0 1.3 collective-permute-start
  5.3 0.7 and_select_fusion.1
  6.2 4.9 %copy.25 = f32[4,8,64,512]{3,0,2,1:T(4,128)S(1)} copy(f32[4,8,64,512]{3,2,1,0:T(8,128)} %param.8) | data formatting | bytes 8388608 | tf_op args[0]
  11.2 1.9 copy-done.2
  13.4 8.9 %scatter-add.4 = f32[4,8,64,512]{3,0,2,1:T(4,128)} dynamic-update-slice(f32[4,8,64,512]{3,0,2,1:T(4,128)} %copy-done.2, f32[4,8,64,1]{3,0,2,1:T(4,128)S(1)} %slice_add_fusion, s32[]{:T(128)} %constant.100.clone.1, s32[]{:T(128)} %constant.100.clone.1, s32[]{:T(128)} %constant.100.clone.1, s32[]{:T(128)} %constant.100.clone.1) | dynamic-update-slice | bytes 16388 | tf_op jit(solution)/shard_map/scatter-add | solution.py:98
  22.3 1.4 fusion.68
  23.8 1.4 collective-permute-start.1
  25.2 5.8 %collective-permute-start.3 = (f32[4,1,64,512]{3,0,2,1:T(4,128)S(1)}, f32[4,1,64,512]{3,0,2,1:T(4,128)S(1)}, u32[]{:S(2)}, u32[]{:S(2)}) collective-permute-start(f32[4,1,64,512]{3,0,2,1:T(4,128)S(1)} %get-tuple-element.30), channel_id=1, source_target_pairs={{0,4},{4,8},{8,12},{12,16},{16,20},{20,24},{24,28},{1,5},{5,9},{9,... | collective-permute-start | bytes 1572872 | tf_op jit(solution)/shard_map/ppermute | solution.py:15
  31.4 1.3 collective-permute-start.4
  32.7 5.1 %collective-permute-start.6 = (f32[10,1,512]{2,1,0:T(1,128)S(1)}, f32[10,1,512]{2,1,0:T(1,128)S(1)}, u32[]{:S(2)}, u32[]{:S(2)}) collective-permute-start(f32[10,1,512]{2,1,0:T(1,128)S(1)} %get-tuple-element.36), channel_id=1, source_target_pairs={{0,1},{1,2},{2,3},{4,5},{5,6},{6,7},{8,9},{9,10},{10,11},{12,13},{... | collective-permute-start | bytes 61448 | tf_op jit(solution)/shard_map/ppermute | solution.py:15
  37.8 18.0 %convolution_bitcast_fusion.4 = f32[4,4]{0,1:T(4,128)S(1)} fusion(f32[4,8,64,512]{3,0,2,1:T(4,128)S(1)} %copy-done.3), kind=kOutput, calls=%fused_computation.77 | convolution fusion | flops 50331648 | bytes 4194368 | tf_op jit(solution)/shard_map/ixyz,jxyz->ij/dot_general | solution.py:57
  55.8 0.7 select_maximum_fusion.8
  56.6 1.3 collective-permute-start.5
  57.9 4.7 %collective-permute-start.7 = (f32[4,10,1,512]{3,0,2,1:T(4,128)S(1)}, f32[4,10,1,512]{3,0,2,1:T(4,128)S(1)}, u32[]{:S(2)}, u32[]{:S(2)}) collective-permute-start(f32[4,10,1,512]{3,0,2,1:T(4,128)S(1)} %get-tuple-element.26), channel_id=1, source_target_pairs={{0,1},{1,2},{2,3},{4,5},{5,6},{6,7},{8,9},{9,10},{10,11},{12,13},{... | collective-permute-start | bytes 245768 | tf_op jit(solution)/shard_map/ppermute | solution.py:15
  62.7 1.0 multiply_select_fusion.3
  63.7 1.5 collective-permute-done.7
  65.2 11.7 %select_maximum_fusion.4 = f32[4,10,66,514]{3,0,2,1:T(4,128)S(1)} fusion(f32[4,10,1,512]{3,0,2,1:T(4,128)S(1)} %collective-permute-done.5, f32[4,10,1,512]{3,0,2,1:T(4,128)S(1)} %collective-permute-done.7, f32[4,1,64,512]{3,0,2,1:T(4,128)S(1)} %collective-permute-done.1, f32[4,8,64,512]{3,0,2,1:T(4,128)S(1)} %copy-done.3, ...), kind=kLoop, calls=%fused_computation.6 | loop fusion | flops 16283520 | bytes 10834560 | tf_op jit(solution)/shard_map/concatenate | solution.py:19
  77.0 10.1 %fusion.17 = f32[4,8,64,512]{3,0,2,1:T(4,128)S(1)} fusion(f32[4,8,64,512]{3,0,2,1:T(4,128)S(1)} %copy-done.3, f32[4,10,66,514]{3,0,2,1:T(4,128)S(1)} %select_maximum_fusion.4, f32[4,10,1,512]{3,0,2,1:T(4,128)S(1)} %collective-permute-done.7, f32[4,1,64,512]{3,0,2,1:T(4,128)S(1)} %collective-permute-done.1, f32[4,1,64,512]{3,0,2,1:T(4,128)S(1)} %collective-permute-done.3, ...), kind=kLoop, calls=%fused_computation.38 | loop fusion | flops 26214400 | bytes 24281088 | tf_op jit(solution)/shard_map/add | solution.py:52
  87.1 2.0 copy-done.6
  89.1 18.3 %convolution_bitcast_fusion.5 = f32[4,4]{0,1:T(4,128)S(1)} fusion(f32[4,8,64,512]{3,0,2,1:T(4,128)S(1)} %copy-done.3, f32[4,8,64,512]{3,0,2,1:T(4,128)S(1)} %fusion.17), kind=kOutput, calls=%fused_computation.78 | convolution fusion | flops 50331648 | bytes 8388672 | tf_op jit(solution)/shard_map/ixyz,jxyz->ij/dot_general | solution.py:57
  107.3 41.2 %all-reduce.4 = (f32[4,4]{0,1:T(4,128)S(1)}, f32[4,4]{0,1:T(4,128)S(1)}) all-reduce(f32[4,4]{0,1:T(4,128)S(1)} %convolution_bitcast_fusion.4, f32[4,4]{0,1:T(4,128)S(1)} %convolution_bitcast_fusion.5), channel_id=1, replica_groups=mesh['gx'=8,'gy'=4] {'gx','gy'}, use_global_device_ids=true, to_apply=%region_3.5 | all-reduce | flops 32 | bytes 256 | tf_op jit(solution)/shard_map/psum | solution.py:75
  149.2 0.7 compare_reduce_fusion.1
  150.2 0.6 compare_reduce_fusion.2
  152.1 10.1 %convolution_subtract_fusion = f32[4,8,64,512]{3,0,2,1:T(4,128)S(1)} fusion(f32[4,8,64,512]{3,0,2,1:T(4,128)} %scatter-add.4, f32[4,4,1,1]{0,1,3,2:T(4,128)S(1)} %convolution_bitcast_fusion.3, f32[4,8,64,512]{3,0,2,1:T(4,128)} %copy-done.6), kind=kOutput, calls=%fused_computation.67 | convolution fusion | flops 51380224 | bytes 12582976 | tf_op jit(solution)/shard_map/ij,ixyz->jxyz/dot_general | solution.py:61
  162.3 1.3 collective-permute-start.8
  163.6 3.5 %collective-permute-start.9 = (f32[4,1,64,512]{3,0,2,1:T(4,128)S(1)}, f32[4,1,64,512]{3,0,2,1:T(4,128)S(1)}, u32[]{:S(2)}, u32[]{:S(2)}) collective-permute-start(f32[4,1,64,512]{3,0,2,1:T(4,128)S(1)} %get-tuple-element.28), channel_id=1, source_target_pairs={{0,4},{4,8},{8,12},{12,16},{16,20},{20,24},{24,28},{1,5},{5,9},{9,... | collective-permute-start | bytes 1572872 | tf_op jit(solution)/shard_map/ppermute | solution.py:15
  167.1 19.1 %convolution_bitcast_fusion.1 = f32[4,4]{1,0:T(4,128)S(1)} fusion(f32[4,8,64,512]{3,0,2,1:T(4,128)S(1)} %convolution_subtract_fusion), kind=kOutput, calls=%fused_computation.74 | convolution fusion | flops 50331648 | bytes 4194368 | tf_op jit(solution)/shard_map/ixyz,jxyz->ij/dot_general | solution.py:57
  186.3 1.3 collective-permute-start.10
  187.6 4.6 %collective-permute-start.11 = (f32[4,10,1,512]{3,0,2,1:T(4,128)S(1)}, f32[4,10,1,512]{3,0,2,1:T(4,128)S(1)}, u32[]{:S(2)}, u32[]{:S(2)}) collective-permute-start(f32[4,10,1,512]{3,0,2,1:T(4,128)S(1)} %get-tuple-element.24), channel_id=1, source_target_pairs={{0,1},{1,2},{2,3},{4,5},{5,6},{6,7},{8,9},{9,10},{10,11},{12,13},{... | collective-permute-start | bytes 245768 | tf_op jit(solution)/shard_map/ppermute | solution.py:15
  192.2 0.6 fusion.48
  192.8 1.5 collective-permute-done.11
  194.4 11.7 %select_maximum_fusion = f32[4,10,66,514]{3,0,2,1:T(4,128)S(1)} fusion(f32[4,10,1,512]{3,0,2,1:T(4,128)S(1)} %collective-permute-done.10, f32[4,10,1,512]{3,0,2,1:T(4,128)S(1)} %collective-permute-done.11, f32[4,1,64,512]{3,0,2,1:T(4,128)S(1)} %collective-permute-done.8, f32[4,8,64,512]{3,0,2,1:T(4,128)S(1)} %convolution_subtract_fusion, ...), kind=kLoop, calls=%fused_computation.2 | loop fusion | flops 16283520 | bytes 10834560 | tf_op jit(solution)/shard_map/concatenate | solution.py:19
  206.1 10.1 %fusion.2 = f32[4,8,64,512]{3,0,2,1:T(4,128)S(1)} fusion(f32[4,8,64,512]{3,0,2,1:T(4,128)S(1)} %convolution_subtract_fusion, f32[4,10,66,514]{3,0,2,1:T(4,128)S(1)} %select_maximum_fusion, f32[4,10,1,512]{3,0,2,1:T(4,128)S(1)} %collective-permute-done.11, f32[4,1,64,512]{3,0,2,1:T(4,128)S(1)} %collective-permute-done.8, ...), kind=kLoop, calls=%fused_computation.13 | loop fusion | flops 26214400 | bytes 24281088 | tf_op jit(solution)/shard_map/add | solution.py:52
  216.2 2.0 copy-done.7
  218.2 18.3 %convolution_bitcast_fusion.2 = f32[4,4]{0,1:T(4,128)S(1)} fusion(f32[4,8,64,512]{3,0,2,1:T(4,128)S(1)} %convolution_subtract_fusion, f32[4,8,64,512]{3,0,2,1:T(4,128)S(1)} %fusion.2), kind=kOutput, calls=%fused_computation.75 | convolution fusion | flops 50331648 | bytes 8388672 | tf_op jit(solution)/shard_map/ixyz,jxyz->ij/dot_general | solution.py:57
  236.8 41.9 %all-reduce.3 = (f32[4,4]{1,0:T(4,128)S(1)}, f32[4,4]{0,1:T(4,128)S(1)}) all-reduce(f32[4,4]{1,0:T(4,128)S(1)} %convolution_bitcast_fusion.1, f32[4,4]{0,1:T(4,128)S(1)} %convolution_bitcast_fusion.2), channel_id=1, replica_groups=mesh['gx'=8,'gy'=4] {'gx','gy'}, use_global_device_ids=true, to_apply=%region_5.8 | all-reduce | flops 32 | bytes 256 | tf_op jit(solution)/shard_map/psum | solution.py:75
  279.1 11.5 %fusion.60 = f32[4,8,64,512]{3,0,2,1:T(4,128)} fusion(f32[4,8,64,512]{3,0,2,1:T(4,128)} %copy-done.6, f32[4,4]{1,0:T(4,128)S(1)} %fusion.55), kind=kOutput, calls=%fused_computation.122 | convolution fusion | flops 50331648 | bytes 8388672 | tf_op jit(solution)/shard_map/ij,ixyz->jxyz/dot_general | solution.py:61
  290.7 10.3 %fusion.62 = f32[4,8,64,512]{3,0,2,1:T(4,128)} fusion(f32[4,8,64,512]{3,0,2,1:T(4,128)S(1)} %copy-done.4, f32[4,4]{1,0:T(4,128)S(1)} %fusion.55), kind=kOutput, calls=%fused_computation.124 | convolution fusion | flops 50331648 | bytes 8388672 | tf_op jit(solution)/shard_map/ij,ixyz->jxyz/dot_general | solution.py:61
  301.7 0.6 compare_reduce_fusion
  302.4 0.6 fusion.49
  303.8 11.5 %fusion.36 = f32[4,8,64,512]{3,0,2,1:T(4,128)S(1)} fusion(f32[4,8,64,512]{3,0,2,1:T(4,128)} %copy-done, f32[4,4,1,1]{0,1,3,2:T(4,128)S(1)} %convolution_bitcast_fusion, f32[4,8,64,512]{3,0,2,1:T(4,128)} %copy-done.7, f32[4,8,64,512]{3,0,2,1:T(4,128)} %fusion.60), kind=kOutput, calls=%fused_computation.72 | convolution fusion | flops 52428800 | bytes 16777280 | tf_op jit(solution)/shard_map/ij,ixyz->jxyz/dot_general | solution.py:61
  315.3 3.4 %copy.41 = f32[4,8,64,512]{3,2,1,0:T(8,128)} copy(f32[4,8,64,512]{3,0,2,1:T(4,128)S(1)} %fusion.36) | data formatting | bytes 8388608
  318.7 1.5 copy-done.8
  320.3 8.1 %fusion.33 = f32[4,8,64,512]{3,0,2,1:T(4,128)S(1)} fusion(f32[4,4,1,1]{0,1,3,2:T(4,128)S(1)} %convolution_bitcast_fusion, f32[4,8,64,512]{3,0,2,1:T(4,128)S(1)} %copy-done.1, f32[4,8,64,512]{3,0,2,1:T(4,128)S(1)} %copy-done.8), kind=kOutput, calls=%fused_computation.63 | convolution fusion | flops 51380224 | bytes 12582976 | tf_op jit(solution)/shard_map/ij,ixyz->jxyz/dot_general | solution.py:61
  328.4 8.5 %convolution_add_fusion = f32[4,8,64,512]{3,0,2,1:T(4,128)S(1)} fusion(f32[4,8,64,512]{3,0,2,1:T(4,128)S(1)} %fusion.33, f32[4,4,1,1]{0,1,3,2:T(4,128)S(1)} %convolution_bitcast_fusion.3, f32[4,8,64,512]{3,0,2,1:T(4,128)S(1)} %copy-done.5), kind=kOutput, calls=%fused_computation.68 | convolution fusion | flops 51380224 | bytes 12582976 | tf_op jit(solution)/shard_map/ij,ixyz->jxyz/dot_general | solution.py:61
  336.9 3.3 copy.40
  (76 shorter events, 5.8 us)
Async XLA Ops:
  1.6 29.4 %collective-permute-start.2 = (f32[1,64,512]{2,1,0:T(8,128)S(1)}, f32[1,64,512]{2,1,0:T(8,128)S(1)}, u32[]{:S(2)}, u32[]{:S(2)}) collective-permute-start(f32[1,64,512]{2,1,0:T(8,128)S(1)} %get-tuple-element.44), channel_id=1, source_target_pairs={{0,4},{4,8},{8,12},{12,16},{16,20},{20,24},{24,28},{1,5},{5,9},{9,... | collective-permute-start | bytes 393224 | tf_op jit(solution)/shard_map/ppermute | solution.py:15
  4.0 27.0 %collective-permute-start = (f32[1,64,512]{2,1,0:T(8,128)S(1)}, f32[1,64,512]{2,1,0:T(8,128)S(1)}, u32[]{:S(2)}, u32[]{:S(2)}) collective-permute-start(f32[1,64,512]{2,1,0:T(8,128)S(1)} %get-tuple-element.43), channel_id=1, source_target_pairs={{4,0},{8,4},{12,8},{16,12},{20,16},{24,20},{28,24},{5,1},{9,5},{13... | collective-permute-start | bytes 393224 | tf_op jit(solution)/shard_map/ppermute | solution.py:18
  11.1 2.0 copy-start.2
  11.1 19.9 %copy-start.15 = (f32[8,64,512]{2,1,0:T(8,128)S(1)}, f32[8,64,512]{2,1,0:T(8,128)}, u32[]{:S(2)}) copy-start(f32[8,64,512]{2,1,0:T(8,128)} %param.9) | copy-start | bytes 3145732
  22.3 15.5 %copy-start.3 = (f32[4,8,64,512]{3,0,2,1:T(4,128)S(1)}, f32[4,8,64,512]{3,0,2,1:T(4,128)}, u32[]{:S(2)}) copy-start(f32[4,8,64,512]{3,0,2,1:T(4,128)} %scatter-add.4) | copy-start | bytes 12582916
  23.8 32.8 %collective-permute-start.1 = (f32[4,1,64,512]{3,0,2,1:T(4,128)S(1)}, f32[4,1,64,512]{3,0,2,1:T(4,128)S(1)}, u32[]{:S(2)}, u32[]{:S(2)}) collective-permute-start(f32[4,1,64,512]{3,0,2,1:T(4,128)S(1)} %get-tuple-element.31), channel_id=1, source_target_pairs={{4,0},{8,4},{12,8},{16,12},{20,16},{24,20},{28,24},{5,1},{9,5},{13... | collective-permute-start | bytes 1572872 | tf_op jit(solution)/shard_map/ppermute | solution.py:18
  25.2 31.4 %collective-permute-start.3 = (f32[4,1,64,512]{3,0,2,1:T(4,128)S(1)}, f32[4,1,64,512]{3,0,2,1:T(4,128)S(1)}, u32[]{:S(2)}, u32[]{:S(2)}) collective-permute-start(f32[4,1,64,512]{3,0,2,1:T(4,128)S(1)} %get-tuple-element.30), channel_id=1, source_target_pairs={{0,4},{4,8},{8,12},{12,16},{16,20},{20,24},{24,28},{1,5},{5,9},{9,... | collective-permute-start | bytes 1572872 | tf_op jit(solution)/shard_map/ppermute | solution.py:15
  31.4 24.4 %collective-permute-start.4 = (f32[10,1,512]{2,1,0:T(1,128)S(1)}, f32[10,1,512]{2,1,0:T(1,128)S(1)}, u32[]{:S(2)}, u32[]{:S(2)}) collective-permute-start(f32[10,1,512]{2,1,0:T(1,128)S(1)} %get-tuple-element.37), channel_id=1, source_target_pairs={{1,0},{2,1},{3,2},{5,4},{6,5},{7,6},{9,8},{10,9},{11,10},{13,12},{... | collective-permute-start | bytes 61448 | tf_op jit(solution)/shard_map/ppermute | solution.py:18
  32.7 23.1 %collective-permute-start.6 = (f32[10,1,512]{2,1,0:T(1,128)S(1)}, f32[10,1,512]{2,1,0:T(1,128)S(1)}, u32[]{:S(2)}, u32[]{:S(2)}) collective-permute-start(f32[10,1,512]{2,1,0:T(1,128)S(1)} %get-tuple-element.36), channel_id=1, source_target_pairs={{0,1},{1,2},{2,3},{4,5},{5,6},{6,7},{8,9},{9,10},{10,11},{12,13},{... | collective-permute-start | bytes 61448 | tf_op jit(solution)/shard_map/ppermute | solution.py:15
  55.8 6.9 %copy-start.16 = (f32[8,64,512]{2,1,0:T(8,128)S(1)}, f32[8,64,512]{2,1,0:T(8,128)}, u32[]{:S(2)}) copy-start(f32[8,64,512]{2,1,0:T(8,128)} %param.9) | copy-start | bytes 3145732
  56.6 7.1 %collective-permute-start.5 = (f32[4,10,1,512]{3,0,2,1:T(4,128)S(1)}, f32[4,10,1,512]{3,0,2,1:T(4,128)S(1)}, u32[]{:S(2)}, u32[]{:S(2)}) collective-permute-start(f32[4,10,1,512]{3,0,2,1:T(4,128)S(1)} %get-tuple-element.27), channel_id=1, source_target_pairs={{1,0},{2,1},{3,2},{5,4},{6,5},{7,6},{9,8},{10,9},{11,10},{13,12},{... | collective-permute-start | bytes 245768 | tf_op jit(solution)/shard_map/ppermute | solution.py:18
  57.9 7.3 %collective-permute-start.7 = (f32[4,10,1,512]{3,0,2,1:T(4,128)S(1)}, f32[4,10,1,512]{3,0,2,1:T(4,128)S(1)}, u32[]{:S(2)}, u32[]{:S(2)}) collective-permute-start(f32[4,10,1,512]{3,0,2,1:T(4,128)S(1)} %get-tuple-element.26), channel_id=1, source_target_pairs={{0,1},{1,2},{2,3},{4,5},{5,6},{6,7},{8,9},{9,10},{10,11},{12,13},{... | collective-permute-start | bytes 245768 | tf_op jit(solution)/shard_map/ppermute | solution.py:15
  63.7 13.2 %copy-start.9 = (f32[8,64,512]{2,1,0:T(8,128)}, f32[8,64,512]{2,1,0:T(8,128)S(1)}, u32[]{:S(2)}) copy-start(f32[8,64,512]{2,1,0:T(8,128)S(1)} %get-tuple-element.35) | copy-start | bytes 3145732
  63.7 13.2 %copy-start.11 = (f32[8,64,512]{2,1,0:T(8,128)}, f32[8,64,512]{2,1,0:T(8,128)S(1)}, u32[]{:S(2)}) copy-start(f32[8,64,512]{2,1,0:T(8,128)S(1)} %get-tuple-element.41) | copy-start | bytes 3145732
  63.7 13.2 %copy-start.13 = (f32[8,64,512]{2,1,0:T(8,128)}, f32[8,64,512]{2,1,0:T(8,128)S(1)}, u32[]{:S(2)}) copy-start(f32[8,64,512]{2,1,0:T(8,128)S(1)} %get-tuple-element.42) | copy-start | bytes 3145732
  87.1 2.0 copy-start.6
  162.3 54.0 %copy-start = (f32[4,8,64,512]{3,0,2,1:T(4,128)}, f32[4,8,64,512]{3,0,2,1:T(4,128)S(1)}, u32[]{:S(2)}) copy-start(f32[4,8,64,512]{3,0,2,1:T(4,128)S(1)} %convolution_subtract_fusion) | copy-start | bytes 12582916
  162.3 23.9 %collective-permute-start.8 = (f32[4,1,64,512]{3,0,2,1:T(4,128)S(1)}, f32[4,1,64,512]{3,0,2,1:T(4,128)S(1)}, u32[]{:S(2)}, u32[]{:S(2)}) collective-permute-start(f32[4,1,64,512]{3,0,2,1:T(4,128)S(1)} %get-tuple-element.29), channel_id=1, source_target_pairs={{4,0},{8,4},{12,8},{16,12},{20,16},{24,20},{28,24},{5,1},{9,5},{13... | collective-permute-start | bytes 1572872 | tf_op jit(solution)/shard_map/ppermute | solution.py:18
  163.6 22.6 %collective-permute-start.9 = (f32[4,1,64,512]{3,0,2,1:T(4,128)S(1)}, f32[4,1,64,512]{3,0,2,1:T(4,128)S(1)}, u32[]{:S(2)}, u32[]{:S(2)}) collective-permute-start(f32[4,1,64,512]{3,0,2,1:T(4,128)S(1)} %get-tuple-element.28), channel_id=1, source_target_pairs={{0,4},{4,8},{8,12},{12,16},{16,20},{20,24},{24,28},{1,5},{5,9},{9,... | collective-permute-start | bytes 1572872 | tf_op jit(solution)/shard_map/ppermute | solution.py:15
  186.3 6.5 %collective-permute-start.10 = (f32[4,10,1,512]{3,0,2,1:T(4,128)S(1)}, f32[4,10,1,512]{3,0,2,1:T(4,128)S(1)}, u32[]{:S(2)}, u32[]{:S(2)}) collective-permute-start(f32[4,10,1,512]{3,0,2,1:T(4,128)S(1)} %get-tuple-element.25), channel_id=1, source_target_pairs={{1,0},{2,1},{3,2},{5,4},{6,5},{7,6},{9,8},{10,9},{11,10},{13,12},{... | collective-permute-start | bytes 245768 | tf_op jit(solution)/shard_map/ppermute | solution.py:18
  187.6 6.8 %collective-permute-start.11 = (f32[4,10,1,512]{3,0,2,1:T(4,128)S(1)}, f32[4,10,1,512]{3,0,2,1:T(4,128)S(1)}, u32[]{:S(2)}, u32[]{:S(2)}) collective-permute-start(f32[4,10,1,512]{3,0,2,1:T(4,128)S(1)} %get-tuple-element.24), channel_id=1, source_target_pairs={{0,1},{1,2},{2,3},{4,5},{5,6},{6,7},{8,9},{9,10},{10,11},{12,13},{... | collective-permute-start | bytes 245768 | tf_op jit(solution)/shard_map/ppermute | solution.py:15
  192.8 13.3 %copy-start.10 = (f32[8,64,512]{2,1,0:T(8,128)S(1)}, f32[8,64,512]{2,1,0:T(8,128)}, u32[]{:S(2)}) copy-start(f32[8,64,512]{2,1,0:T(8,128)} %copy-done.9) | copy-start | bytes 3145732
  192.8 13.3 %copy-start.12 = (f32[8,64,512]{2,1,0:T(8,128)S(1)}, f32[8,64,512]{2,1,0:T(8,128)}, u32[]{:S(2)}) copy-start(f32[8,64,512]{2,1,0:T(8,128)} %copy-done.11) | copy-start | bytes 3145732
  192.8 13.3 %copy-start.14 = (f32[8,64,512]{2,1,0:T(8,128)S(1)}, f32[8,64,512]{2,1,0:T(8,128)}, u32[]{:S(2)}) copy-start(f32[8,64,512]{2,1,0:T(8,128)} %copy-done.13) | copy-start | bytes 3145732
  216.2 2.0 copy-start.7
  279.1 11.7 %copy-start.4 = (f32[4,8,64,512]{3,0,2,1:T(4,128)S(1)}, f32[4,8,64,512]{3,0,2,1:T(4,128)}, u32[]{:S(2)}) copy-start(f32[4,8,64,512]{3,0,2,1:T(4,128)} %scatter-add.4) | copy-start | bytes 12582916
  315.3 3.4 %copy-start.1 = (f32[4,8,64,512]{3,0,2,1:T(4,128)S(1)}, f32[4,8,64,512]{3,0,2,1:T(4,128)}, u32[]{:S(2)}) copy-start(f32[4,8,64,512]{3,0,2,1:T(4,128)} %copy-done) | copy-start | bytes 12582916
  315.3 5.0 %copy-start.8 = (f32[4,8,64,512]{3,0,2,1:T(4,128)S(1)}, f32[4,8,64,512]{3,0,2,1:T(4,128)}, u32[]{:S(2)}) copy-start(f32[4,8,64,512]{3,0,2,1:T(4,128)} %fusion.62) | copy-start | bytes 12582916
  320.3 8.1 %copy-start.5 = (f32[4,8,64,512]{3,0,2,1:T(4,128)S(1)}, f32[4,8,64,512]{3,0,2,1:T(4,128)}, u32[]{:S(2)}) copy-start(f32[4,8,64,512]{3,0,2,1:T(4,128)} %scatter-add.4) | copy-start | bytes 12582916
where the time goes:
time: 346 us; the launch traced here: 341 us
  matrix products  135 us (39%)
  blocking collectives  83.2 us (24%)
  other arithmetic  52.9 us (15%)
  starting transfers between devices  33.9 us (10%)
  local copies, waits for them, and re-layouts  30.9 us (9%)
    psum x2, blocking collectives, paired_products(): lax.psum((gram(residual, residual), gram(residual, image)), ('gx', 'gy'))  83.2 us
    dot_general x4, matrix products, gram(): jnp.einsum('ixyz,jxyz->ij', left, right, precision=lax.Precision.HIGHEST)  73.6 us
    dot_general x6, matrix products, combine(): jnp.einsum('ij,ixyz->jxyz', matrix, block, precision=lax.Precision.HIGHEST)  60 us
    ppermute x6, starting transfers between devices, with_halo(): lax.ppermute(lax.slice_in_dim(block, block.shape[dim] - width, None, axis...  26 us
    concatenate x5, other arithmetic, with_halo(): block = jnp.concatenate([low, block, high], axis=dim)  24.3 us
    add x2, other arithmetic, apply_operator(): total = total + coeff[None] * (center - other)  20.2 us
    unnamed x38, local copies, waits for them, and re-layouts  19.1 us
    scatter-add x1, local copies, waits for them, and re-layouts, shards(): right_side = adjoint_source.at[:, :, :, 0].add(spike)  8.89 us
  transfers between devices with their start and end apart: 12, of which 2 were waited for; matrix products, arithmetic and copies ran while one was open for 17% of the time, Pallas kernels for 0%

commit v1 on v0

--- a/solution.py
+++ b/solution.py
@@ -72,7 +72,7 @@
 
 
 def paired_products(residual, image):
-    return lax.psum((gram(residual, residual), gram(residual, image)), ("gx", "gy"))
+    return lax.psum(lax.psum((gram(residual, residual), gram(residual, image)), "gx"), "gy")
 
 
 def shards(adjoint_source, conductivity, electrodes):

time: 346 us -> 310 us (0.90)
  blocking collectives: 83.2 us -> 47.4 us
    psum x2 -> x4, blocking collectives: 83.2 us -> 47.4 us  [the longest x2 23.8 us: paired_products(): lax.psum(lax.psum((gram(residual, residual), gram(residual, image)), 'gx'...]
  transfers between devices with their start and end apart: 12 -> 12, of which waited for: 2 -> 2; matrix products, arithmetic and copies ran while one was open for 17% -> 19% of each run, Pallas kernels for 0% -> 0%
where the time goes in v1:
time: 310 us; the launch traced here: 304 us
  matrix products  135 us (44%)
  other arithmetic  53.1 us (17%)
  blocking collectives  47.4 us (15%)
  starting transfers between devices  33.8 us (11%)
  local copies, waits for them, and re-layouts  30.9 us (10%)
    dot_general x4, matrix products, gram(): jnp.einsum('ixyz,jxyz->ij', left, right, precision=lax.Precision.HIGHEST)  73.6 us
    dot_general x6, matrix products, combine(): jnp.einsum('ij,ixyz->jxyz', matrix, block, precision=lax.Precision.HIGHEST)  59.7 us
    ppermute x6, starting transfers between devices, with_halo(): lax.ppermute(lax.slice_in_dim(block, block.shape[dim] - width, None, axis...  25.9 us
    concatenate x5, other arithmetic, with_halo(): block = jnp.concatenate([low, block, high], axis=dim)  24.3 us
    psum x2, blocking collectives, paired_products(): lax.psum(lax.psum((gram(residual, residual), gram(residual, image)), 'gx'...  23.8 us
    psum x2, blocking collectives, paired_products(): lax.psum((gram(residual, residual), gram(residual, image)), 'gx')  23.6 us
    add x2, other arithmetic, apply_operator(): total = total + coeff[None] * (center - other)  20.2 us
    unnamed x38, local copies, waits for them, and re-layouts  19.1 us
  transfers between devices with their start and end apart: 12, of which 2 were waited for; matrix products, arithmetic and copies ran while one was open for 19% of the time, Pallas kernels for 0%

profile of v1, /device:TPU:0, one launch (start us, length us, event | category | flops | bytes accessed | tf_op | source)
XLA Modules:
  0.0 304.5 jit_solution(7033553498119721207)
XLA Ops:
  0.6 1.0 fusion.70
  1.6 2.4 collective-permute-start.2
  4.0 1.3 collective-permute-start
  5.3 0.7 and_select_fusion.1
  6.2 4.9 %copy.25 = f32[4,8,64,512]{3,0,2,1:T(4,128)S(1)} copy(f32[4,8,64,512]{3,2,1,0:T(8,128)} %param.8) | data formatting | bytes 8388608 | tf_op args[0]
  11.2 1.9 copy-done.2
  13.4 8.9 %scatter-add.4 = f32[4,8,64,512]{3,0,2,1:T(4,128)} dynamic-update-slice(f32[4,8,64,512]{3,0,2,1:T(4,128)} %copy-done.2, f32[4,8,64,1]{3,0,2,1:T(4,128)S(1)} %slice_add_fusion, s32[]{:T(128)} %constant.100.clone.1, s32[]{:T(128)} %constant.100.clone.1, s32[]{:T(128)} %constant.100.clone.1, s32[]{:T(128)} %constant.100.clone.1) | dynamic-update-slice | bytes 16388 | tf_op jit(solution)/shard_map/scatter-add | solution.py:98
  22.3 1.4 fusion.68
  23.8 1.4 collective-permute-start.1
  25.2 5.8 %collective-permute-start.3 = (f32[4,1,64,512]{3,0,2,1:T(4,128)S(1)}, f32[4,1,64,512]{3,0,2,1:T(4,128)S(1)}, u32[]{:S(2)}, u32[]{:S(2)}) collective-permute-start(f32[4,1,64,512]{3,0,2,1:T(4,128)S(1)} %get-tuple-element.34), channel_id=1, source_target_pairs={{0,4},{4,8},{8,12},{12,16},{16,20},{20,24},{24,28},{1,5},{5,9},{9,... | collective-permute-start | bytes 1572872 | tf_op jit(solution)/shard_map/ppermute | solution.py:15
  31.4 1.3 collective-permute-start.4
  32.7 5.0 %collective-permute-start.6 = (f32[10,1,512]{2,1,0:T(1,128)S(1)}, f32[10,1,512]{2,1,0:T(1,128)S(1)}, u32[]{:S(2)}, u32[]{:S(2)}) collective-permute-start(f32[10,1,512]{2,1,0:T(1,128)S(1)} %get-tuple-element.40), channel_id=1, source_target_pairs={{0,1},{1,2},{2,3},{4,5},{5,6},{6,7},{8,9},{9,10},{10,11},{12,13},{... | collective-permute-start | bytes 61448 | tf_op jit(solution)/shard_map/ppermute | solution.py:15
  37.8 18.0 %convolution_bitcast_fusion.4 = f32[4,4]{0,1:T(4,128)S(1)} fusion(f32[4,8,64,512]{3,0,2,1:T(4,128)S(1)} %copy-done.3), kind=kOutput, calls=%fused_computation.77 | convolution fusion | flops 50331648 | bytes 4194368 | tf_op jit(solution)/shard_map/ixyz,jxyz->ij/dot_general | solution.py:57
  55.7 0.7 select_maximum_fusion.8
  56.6 1.3 collective-permute-start.5
  57.9 4.7 %collective-permute-start.7 = (f32[4,10,1,512]{3,0,2,1:T(4,128)S(1)}, f32[4,10,1,512]{3,0,2,1:T(4,128)S(1)}, u32[]{:S(2)}, u32[]{:S(2)}) collective-permute-start(f32[4,10,1,512]{3,0,2,1:T(4,128)S(1)} %get-tuple-element.30), channel_id=1, source_target_pairs={{0,1},{1,2},{2,3},{4,5},{5,6},{6,7},{8,9},{9,10},{10,11},{12,13},{... | collective-permute-start | bytes 245768 | tf_op jit(solution)/shard_map/ppermute | solution.py:15
  62.6 1.0 multiply_select_fusion.3
  63.7 1.5 collective-permute-done.7
  65.1 11.7 %select_maximum_fusion.4 = f32[4,10,66,514]{3,0,2,1:T(4,128)S(1)} fusion(f32[4,10,1,512]{3,0,2,1:T(4,128)S(1)} %collective-permute-done.5, f32[4,10,1,512]{3,0,2,1:T(4,128)S(1)} %collective-permute-done.7, f32[4,1,64,512]{3,0,2,1:T(4,128)S(1)} %collective-permute-done.1, f32[4,8,64,512]{3,0,2,1:T(4,128)S(1)} %copy-done.3, ...), kind=kLoop, calls=%fused_computation.6 | loop fusion | flops 16283520 | bytes 10834560 | tf_op jit(solution)/shard_map/concatenate | solution.py:19
  76.9 10.1 %fusion.17 = f32[4,8,64,512]{3,0,2,1:T(4,128)S(1)} fusion(f32[4,8,64,512]{3,0,2,1:T(4,128)S(1)} %copy-done.3, f32[4,10,66,514]{3,0,2,1:T(4,128)S(1)} %select_maximum_fusion.4, f32[4,10,1,512]{3,0,2,1:T(4,128)S(1)} %collective-permute-done.7, f32[4,1,64,512]{3,0,2,1:T(4,128)S(1)} %collective-permute-done.1, f32[4,1,64,512]{3,0,2,1:T(4,128)S(1)} %collective-permute-done.3, ...), kind=kLoop, calls=%fused_computation.38 | loop fusion | flops 26214400 | bytes 24281088 | tf_op jit(solution)/shard_map/add | solution.py:52
  87.0 2.0 copy-done.6
  89.0 18.3 %convolution_bitcast_fusion.5 = f32[4,4]{0,1:T(4,128)S(1)} fusion(f32[4,8,64,512]{3,0,2,1:T(4,128)S(1)} %copy-done.3, f32[4,8,64,512]{3,0,2,1:T(4,128)S(1)} %fusion.17), kind=kOutput, calls=%fused_computation.78 | convolution fusion | flops 50331648 | bytes 8388672 | tf_op jit(solution)/shard_map/ixyz,jxyz->ij/dot_general | solution.py:57
  107.3 11.8 %all-reduce.4 = (f32[4,4]{0,1:T(4,128)S(1)}, f32[4,4]{0,1:T(4,128)S(1)}) all-reduce(f32[4,4]{0,1:T(4,128)S(1)} %convolution_bitcast_fusion.4, f32[4,4]{0,1:T(4,128)S(1)} %convolution_bitcast_fusion.5), channel_id=1, replica_groups=mesh['gx'=8,'gy'=4] {'gx'}, use_global_device_ids=true, to_apply=%region_4.6 | all-reduce | flops 32 | bytes 256 | tf_op jit(solution)/shard_map/psum | solution.py:75
  119.1 12.9 %all-reduce.6 = (f32[4,4]{0,1:T(4,128)S(1)}, f32[4,4]{0,1:T(4,128)S(1)}) all-reduce(f32[4,4]{0,1:T(4,128)S(1)} %get-tuple-element.22, f32[4,4]{0,1:T(4,128)S(1)} %get-tuple-element.23), channel_id=1, replica_groups=mesh['gx'=8,'gy'=4] {'gy'}, use_global_device_ids=true, to_apply=%region_5.7 | all-reduce | flops 32 | bytes 256 | tf_op jit(solution)/shard_map/psum | solution.py:75
  132.5 0.7 compare_reduce_fusion.1
  133.6 0.6 compare_reduce_fusion.2
  135.6 10.1 %convolution_subtract_fusion = f32[4,8,64,512]{3,0,2,1:T(4,128)S(1)} fusion(f32[4,8,64,512]{3,0,2,1:T(4,128)} %scatter-add.4, f32[4,4,1,1]{0,1,3,2:T(4,128)S(1)} %convolution_bitcast_fusion.3, f32[4,8,64,512]{3,0,2,1:T(4,128)} %copy-done.6), kind=kOutput, calls=%fused_computation.67 | convolution fusion | flops 51380224 | bytes 12582976 | tf_op jit(solution)/shard_map/ij,ixyz->jxyz/dot_general | solution.py:61
  145.8 1.3 collective-permute-start.8
  147.1 3.5 %collective-permute-start.9 = (f32[4,1,64,512]{3,0,2,1:T(4,128)S(1)}, f32[4,1,64,512]{3,0,2,1:T(4,128)S(1)}, u32[]{:S(2)}, u32[]{:S(2)}) collective-permute-start(f32[4,1,64,512]{3,0,2,1:T(4,128)S(1)} %get-tuple-element.32), channel_id=1, source_target_pairs={{0,4},{4,8},{8,12},{12,16},{16,20},{20,24},{24,28},{1,5},{5,9},{9,... | collective-permute-start | bytes 1572872 | tf_op jit(solution)/shard_map/ppermute | solution.py:15
  150.6 19.1 %convolution_bitcast_fusion.1 = f32[4,4]{1,0:T(4,128)S(1)} fusion(f32[4,8,64,512]{3,0,2,1:T(4,128)S(1)} %convolution_subtract_fusion), kind=kOutput, calls=%fused_computation.74 | convolution fusion | flops 50331648 | bytes 4194368 | tf_op jit(solution)/shard_map/ixyz,jxyz->ij/dot_general | solution.py:57
  169.8 1.3 collective-permute-start.10
  171.1 4.6 %collective-permute-start.11 = (f32[4,10,1,512]{3,0,2,1:T(4,128)S(1)}, f32[4,10,1,512]{3,0,2,1:T(4,128)S(1)}, u32[]{:S(2)}, u32[]{:S(2)}) collective-permute-start(f32[4,10,1,512]{3,0,2,1:T(4,128)S(1)} %get-tuple-element.28), channel_id=1, source_target_pairs={{0,1},{1,2},{2,3},{4,5},{5,6},{6,7},{8,9},{9,10},{10,11},{12,13},{... | collective-permute-start | bytes 245768 | tf_op jit(solution)/shard_map/ppermute | solution.py:15
  175.6 0.7 fusion.48
  176.4 1.3 collective-permute-done.11
  177.7 11.7 %select_maximum_fusion = f32[4,10,66,514]{3,0,2,1:T(4,128)S(1)} fusion(f32[4,10,1,512]{3,0,2,1:T(4,128)S(1)} %collective-permute-done.10, f32[4,10,1,512]{3,0,2,1:T(4,128)S(1)} %collective-permute-done.11, f32[4,1,64,512]{3,0,2,1:T(4,128)S(1)} %collective-permute-done.8, f32[4,8,64,512]{3,0,2,1:T(4,128)S(1)} %convolution_subtract_fusion, ...), kind=kLoop, calls=%fused_computation.2 | loop fusion | flops 16283520 | bytes 10834560 | tf_op jit(solution)/shard_map/concatenate | solution.py:19
  189.5 10.1 %fusion.2 = f32[4,8,64,512]{3,0,2,1:T(4,128)S(1)} fusion(f32[4,8,64,512]{3,0,2,1:T(4,128)S(1)} %convolution_subtract_fusion, f32[4,10,66,514]{3,0,2,1:T(4,128)S(1)} %select_maximum_fusion, f32[4,10,1,512]{3,0,2,1:T(4,128)S(1)} %collective-permute-done.11, f32[4,1,64,512]{3,0,2,1:T(4,128)S(1)} %collective-permute-done.8, ...), kind=kLoop, calls=%fused_computation.13 | loop fusion | flops 26214400 | bytes 24281088 | tf_op jit(solution)/shard_map/add | solution.py:52
  199.6 2.0 copy-done.7
  201.5 18.3 %convolution_bitcast_fusion.2 = f32[4,4]{0,1:T(4,128)S(1)} fusion(f32[4,8,64,512]{3,0,2,1:T(4,128)S(1)} %convolution_subtract_fusion, f32[4,8,64,512]{3,0,2,1:T(4,128)S(1)} %fusion.2), kind=kOutput, calls=%fused_computation.75 | convolution fusion | flops 50331648 | bytes 8388672 | tf_op jit(solution)/shard_map/ixyz,jxyz->ij/dot_general | solution.py:57
  220.1 11.8 %all-reduce.3 = (f32[4,4]{1,0:T(4,128)S(1)}, f32[4,4]{0,1:T(4,128)S(1)}) all-reduce(f32[4,4]{1,0:T(4,128)S(1)} %convolution_bitcast_fusion.1, f32[4,4]{0,1:T(4,128)S(1)} %convolution_bitcast_fusion.2), channel_id=1, replica_groups=mesh['gx'=8,'gy'=4] {'gx'}, use_global_device_ids=true, to_apply=%region_8.11 | all-reduce | flops 32 | bytes 256 | tf_op jit(solution)/shard_map/psum | solution.py:75
  231.9 10.9 %all-reduce.5 = (f32[4,4]{1,0:T(4,128)S(1)}, f32[4,4]{0,1:T(4,128)S(1)}) all-reduce(f32[4,4]{1,0:T(4,128)S(1)} %get-tuple-element.20, f32[4,4]{0,1:T(4,128)S(1)} %get-tuple-element.21), channel_id=1, replica_groups=mesh['gx'=8,'gy'=4] {'gy'}, use_global_device_ids=true, to_apply=%region_9.12 | all-reduce | flops 32 | bytes 256 | tf_op jit(solution)/shard_map/psum | solution.py:75
  243.2 11.5 %fusion.60 = f32[4,8,64,512]{3,0,2,1:T(4,128)} fusion(f32[4,8,64,512]{3,0,2,1:T(4,128)} %copy-done.6, f32[4,4]{1,0:T(4,128)S(1)} %fusion.55), kind=kOutput, calls=%fused_computation.122 | convolution fusion | flops 50331648 | bytes 8388672 | tf_op jit(solution)/shard_map/ij,ixyz->jxyz/dot_general | solution.py:61
  254.9 10.3 %fusion.62 = f32[4,8,64,512]{3,0,2,1:T(4,128)} fusion(f32[4,8,64,512]{3,0,2,1:T(4,128)S(1)} %copy-done.4, f32[4,4]{1,0:T(4,128)S(1)} %fusion.55), kind=kOutput, calls=%fused_computation.124 | convolution fusion | flops 50331648 | bytes 8388672 | tf_op jit(solution)/shard_map/ij,ixyz->jxyz/dot_general | solution.py:61
  267.9 11.5 %fusion.36 = f32[4,8,64,512]{3,0,2,1:T(4,128)S(1)} fusion(f32[4,8,64,512]{3,0,2,1:T(4,128)} %copy-done, f32[4,4,1,1]{0,1,3,2:T(4,128)S(1)} %convolution_bitcast_fusion, f32[4,8,64,512]{3,0,2,1:T(4,128)} %copy-done.7, f32[4,8,64,512]{3,0,2,1:T(4,128)} %fusion.60), kind=kOutput, calls=%fused_computation.72 | convolution fusion | flops 52428800 | bytes 16777280 | tf_op jit(solution)/shard_map/ij,ixyz->jxyz/dot_general | solution.py:61
  279.4 3.4 %copy.41 = f32[4,8,64,512]{3,2,1,0:T(8,128)} copy(f32[4,8,64,512]{3,0,2,1:T(4,128)S(1)} %fusion.36) | data formatting | bytes 8388608
  282.8 1.5 copy-done.8
  284.4 8.1 %fusion.33 = f32[4,8,64,512]{3,0,2,1:T(4,128)S(1)} fusion(f32[4,4,1,1]{0,1,3,2:T(4,128)S(1)} %convolution_bitcast_fusion, f32[4,8,64,512]{3,0,2,1:T(4,128)S(1)} %copy-done.1, f32[4,8,64,512]{3,0,2,1:T(4,128)S(1)} %copy-done.8), kind=kOutput, calls=%fused_computation.63 | convolution fusion | flops 51380224 | bytes 12582976 | tf_op jit(solution)/shard_map/ij,ixyz->jxyz/dot_general | solution.py:61
  292.5 8.2 %convolution_add_fusion = f32[4,8,64,512]{3,0,2,1:T(4,128)S(1)} fusion(f32[4,8,64,512]{3,0,2,1:T(4,128)S(1)} %fusion.33, f32[4,4,1,1]{0,1,3,2:T(4,128)S(1)} %convolution_bitcast_fusion.3, f32[4,8,64,512]{3,0,2,1:T(4,128)S(1)} %copy-done.5), kind=kOutput, calls=%fused_computation.68 | convolution fusion | flops 51380224 | bytes 12582976 | tf_op jit(solution)/shard_map/ij,ixyz->jxyz/dot_general | solution.py:61
  300.7 3.3 %copy.40 = f32[4,8,64,512]{3,2,1,0:T(8,128)} copy(f32[4,8,64,512]{3,0,2,1:T(4,128)S(1)} %convolution_add_fusion) | data formatting | bytes 8388608
  (78 shorter events, 7.1 us)
Async XLA Ops:
  1.6 29.4 %collective-permute-start.2 = (f32[1,64,512]{2,1,0:T(8,128)S(1)}, f32[1,64,512]{2,1,0:T(8,128)S(1)}, u32[]{:S(2)}, u32[]{:S(2)}) collective-permute-start(f32[1,64,512]{2,1,0:T(8,128)S(1)} %get-tuple-element.48), channel_id=1, source_target_pairs={{0,4},{4,8},{8,12},{12,16},{16,20},{20,24},{24,28},{1,5},{5,9},{9,... | collective-permute-start | bytes 393224 | tf_op jit(solution)/shard_map/ppermute | solution.py:15
  4.0 27.0 %collective-permute-start = (f32[1,64,512]{2,1,0:T(8,128)S(1)}, f32[1,64,512]{2,1,0:T(8,128)S(1)}, u32[]{:S(2)}, u32[]{:S(2)}) collective-permute-start(f32[1,64,512]{2,1,0:T(8,128)S(1)} %get-tuple-element.47), channel_id=1, source_target_pairs={{4,0},{8,4},{12,8},{16,12},{20,16},{24,20},{28,24},{5,1},{9,5},{13... | collective-permute-start | bytes 393224 | tf_op jit(solution)/shard_map/ppermute | solution.py:18
  11.1 2.0 copy-start.2
  11.1 19.9 %copy-start.15 = (f32[8,64,512]{2,1,0:T(8,128)S(1)}, f32[8,64,512]{2,1,0:T(8,128)}, u32[]{:S(2)}) copy-start(f32[8,64,512]{2,1,0:T(8,128)} %param.9) | copy-start | bytes 3145732
  22.3 15.4 %copy-start.3 = (f32[4,8,64,512]{3,0,2,1:T(4,128)S(1)}, f32[4,8,64,512]{3,0,2,1:T(4,128)}, u32[]{:S(2)}) copy-start(f32[4,8,64,512]{3,0,2,1:T(4,128)} %scatter-add.4) | copy-start | bytes 12582916
  23.8 32.7 %collective-permute-start.1 = (f32[4,1,64,512]{3,0,2,1:T(4,128)S(1)}, f32[4,1,64,512]{3,0,2,1:T(4,128)S(1)}, u32[]{:S(2)}, u32[]{:S(2)}) collective-permute-start(f32[4,1,64,512]{3,0,2,1:T(4,128)S(1)} %get-tuple-element.35), channel_id=1, source_target_pairs={{4,0},{8,4},{12,8},{16,12},{20,16},{24,20},{28,24},{5,1},{9,5},{13... | collective-permute-start | bytes 1572872 | tf_op jit(solution)/shard_map/ppermute | solution.py:18
  25.2 31.3 %collective-permute-start.3 = (f32[4,1,64,512]{3,0,2,1:T(4,128)S(1)}, f32[4,1,64,512]{3,0,2,1:T(4,128)S(1)}, u32[]{:S(2)}, u32[]{:S(2)}) collective-permute-start(f32[4,1,64,512]{3,0,2,1:T(4,128)S(1)} %get-tuple-element.34), channel_id=1, source_target_pairs={{0,4},{4,8},{8,12},{12,16},{16,20},{20,24},{24,28},{1,5},{5,9},{9,... | collective-permute-start | bytes 1572872 | tf_op jit(solution)/shard_map/ppermute | solution.py:15
  31.4 24.3 %collective-permute-start.4 = (f32[10,1,512]{2,1,0:T(1,128)S(1)}, f32[10,1,512]{2,1,0:T(1,128)S(1)}, u32[]{:S(2)}, u32[]{:S(2)}) collective-permute-start(f32[10,1,512]{2,1,0:T(1,128)S(1)} %get-tuple-element.41), channel_id=1, source_target_pairs={{1,0},{2,1},{3,2},{5,4},{6,5},{7,6},{9,8},{10,9},{11,10},{13,12},{... | collective-permute-start | bytes 61448 | tf_op jit(solution)/shard_map/ppermute | solution.py:18
  32.7 23.0 %collective-permute-start.6 = (f32[10,1,512]{2,1,0:T(1,128)S(1)}, f32[10,1,512]{2,1,0:T(1,128)S(1)}, u32[]{:S(2)}, u32[]{:S(2)}) collective-permute-start(f32[10,1,512]{2,1,0:T(1,128)S(1)} %get-tuple-element.40), channel_id=1, source_target_pairs={{0,1},{1,2},{2,3},{4,5},{5,6},{6,7},{8,9},{9,10},{10,11},{12,13},{... | collective-permute-start | bytes 61448 | tf_op jit(solution)/shard_map/ppermute | solution.py:15
  55.7 6.9 %copy-start.16 = (f32[8,64,512]{2,1,0:T(8,128)S(1)}, f32[8,64,512]{2,1,0:T(8,128)}, u32[]{:S(2)}) copy-start(f32[8,64,512]{2,1,0:T(8,128)} %param.9) | copy-start | bytes 3145732
  56.6 7.1 %collective-permute-start.5 = (f32[4,10,1,512]{3,0,2,1:T(4,128)S(1)}, f32[4,10,1,512]{3,0,2,1:T(4,128)S(1)}, u32[]{:S(2)}, u32[]{:S(2)}) collective-permute-start(f32[4,10,1,512]{3,0,2,1:T(4,128)S(1)} %get-tuple-element.31), channel_id=1, source_target_pairs={{1,0},{2,1},{3,2},{5,4},{6,5},{7,6},{9,8},{10,9},{11,10},{13,12},{... | collective-permute-start | bytes 245768 | tf_op jit(solution)/shard_map/ppermute | solution.py:18
  57.9 7.3 %collective-permute-start.7 = (f32[4,10,1,512]{3,0,2,1:T(4,128)S(1)}, f32[4,10,1,512]{3,0,2,1:T(4,128)S(1)}, u32[]{:S(2)}, u32[]{:S(2)}) collective-permute-start(f32[4,10,1,512]{3,0,2,1:T(4,128)S(1)} %get-tuple-element.30), channel_id=1, source_target_pairs={{0,1},{1,2},{2,3},{4,5},{5,6},{6,7},{8,9},{9,10},{10,11},{12,13},{... | collective-permute-start | bytes 245768 | tf_op jit(solution)/shard_map/ppermute | solution.py:15
  63.6 13.2 %copy-start.9 = (f32[8,64,512]{2,1,0:T(8,128)}, f32[8,64,512]{2,1,0:T(8,128)S(1)}, u32[]{:S(2)}) copy-start(f32[8,64,512]{2,1,0:T(8,128)S(1)} %get-tuple-element.39) | copy-start | bytes 3145732
  63.6 13.2 %copy-start.11 = (f32[8,64,512]{2,1,0:T(8,128)}, f32[8,64,512]{2,1,0:T(8,128)S(1)}, u32[]{:S(2)}) copy-start(f32[8,64,512]{2,1,0:T(8,128)S(1)} %get-tuple-element.45) | copy-start | bytes 3145732
  63.7 13.2 %copy-start.13 = (f32[8,64,512]{2,1,0:T(8,128)}, f32[8,64,512]{2,1,0:T(8,128)S(1)}, u32[]{:S(2)}) copy-start(f32[8,64,512]{2,1,0:T(8,128)S(1)} %get-tuple-element.46) | copy-start | bytes 3145732
  87.0 2.0 copy-start.6
  145.7 53.8 %copy-start = (f32[4,8,64,512]{3,0,2,1:T(4,128)}, f32[4,8,64,512]{3,0,2,1:T(4,128)S(1)}, u32[]{:S(2)}) copy-start(f32[4,8,64,512]{3,0,2,1:T(4,128)S(1)} %convolution_subtract_fusion) | copy-start | bytes 12582916
  145.8 23.9 %collective-permute-start.8 = (f32[4,1,64,512]{3,0,2,1:T(4,128)S(1)}, f32[4,1,64,512]{3,0,2,1:T(4,128)S(1)}, u32[]{:S(2)}, u32[]{:S(2)}) collective-permute-start(f32[4,1,64,512]{3,0,2,1:T(4,128)S(1)} %get-tuple-element.33), channel_id=1, source_target_pairs={{4,0},{8,4},{12,8},{16,12},{20,16},{24,20},{28,24},{5,1},{9,5},{13... | collective-permute-start | bytes 1572872 | tf_op jit(solution)/shard_map/ppermute | solution.py:18
  147.1 22.6 %collective-permute-start.9 = (f32[4,1,64,512]{3,0,2,1:T(4,128)S(1)}, f32[4,1,64,512]{3,0,2,1:T(4,128)S(1)}, u32[]{:S(2)}, u32[]{:S(2)}) collective-permute-start(f32[4,1,64,512]{3,0,2,1:T(4,128)S(1)} %get-tuple-element.32), channel_id=1, source_target_pairs={{0,4},{4,8},{8,12},{12,16},{16,20},{20,24},{24,28},{1,5},{5,9},{9,... | collective-permute-start | bytes 1572872 | tf_op jit(solution)/shard_map/ppermute | solution.py:15
  169.8 6.6 %collective-permute-start.10 = (f32[4,10,1,512]{3,0,2,1:T(4,128)S(1)}, f32[4,10,1,512]{3,0,2,1:T(4,128)S(1)}, u32[]{:S(2)}, u32[]{:S(2)}) collective-permute-start(f32[4,10,1,512]{3,0,2,1:T(4,128)S(1)} %get-tuple-element.29), channel_id=1, source_target_pairs={{1,0},{2,1},{3,2},{5,4},{6,5},{7,6},{9,8},{10,9},{11,10},{13,12},{... | collective-permute-start | bytes 245768 | tf_op jit(solution)/shard_map/ppermute | solution.py:18
  171.1 6.6 %collective-permute-start.11 = (f32[4,10,1,512]{3,0,2,1:T(4,128)S(1)}, f32[4,10,1,512]{3,0,2,1:T(4,128)S(1)}, u32[]{:S(2)}, u32[]{:S(2)}) collective-permute-start(f32[4,10,1,512]{3,0,2,1:T(4,128)S(1)} %get-tuple-element.28), channel_id=1, source_target_pairs={{0,1},{1,2},{2,3},{4,5},{5,6},{6,7},{8,9},{9,10},{10,11},{12,13},{... | collective-permute-start | bytes 245768 | tf_op jit(solution)/shard_map/ppermute | solution.py:15
  176.3 13.1 %copy-start.10 = (f32[8,64,512]{2,1,0:T(8,128)S(1)}, f32[8,64,512]{2,1,0:T(8,128)}, u32[]{:S(2)}) copy-start(f32[8,64,512]{2,1,0:T(8,128)} %copy-done.9) | copy-start | bytes 3145732
  176.3 13.1 %copy-start.12 = (f32[8,64,512]{2,1,0:T(8,128)S(1)}, f32[8,64,512]{2,1,0:T(8,128)}, u32[]{:S(2)}) copy-start(f32[8,64,512]{2,1,0:T(8,128)} %copy-done.11) | copy-start | bytes 3145732
  176.4 13.1 %copy-start.14 = (f32[8,64,512]{2,1,0:T(8,128)S(1)}, f32[8,64,512]{2,1,0:T(8,128)}, u32[]{:S(2)}) copy-start(f32[8,64,512]{2,1,0:T(8,128)} %copy-done.13) | copy-start | bytes 3145732
  199.5 2.0 copy-start.7
  243.2 11.7 %copy-start.4 = (f32[4,8,64,512]{3,0,2,1:T(4,128)S(1)}, f32[4,8,64,512]{3,0,2,1:T(4,128)}, u32[]{:S(2)}) copy-start(f32[4,8,64,512]{3,0,2,1:T(4,128)} %scatter-add.4) | copy-start | bytes 12582916
  279.4 3.4 %copy-start.1 = (f32[4,8,64,512]{3,0,2,1:T(4,128)S(1)}, f32[4,8,64,512]{3,0,2,1:T(4,128)}, u32[]{:S(2)}) copy-start(f32[4,8,64,512]{3,0,2,1:T(4,128)} %copy-done) | copy-start | bytes 12582916
  279.4 5.0 %copy-start.8 = (f32[4,8,64,512]{3,0,2,1:T(4,128)S(1)}, f32[4,8,64,512]{3,0,2,1:T(4,128)}, u32[]{:S(2)}) copy-start(f32[4,8,64,512]{3,0,2,1:T(4,128)} %fusion.62) | copy-start | bytes 12582916
  284.4 8.1 %copy-start.5 = (f32[4,8,64,512]{3,0,2,1:T(4,128)S(1)}, f32[4,8,64,512]{3,0,2,1:T(4,128)}, u32[]{:S(2)}) copy-start(f32[4,8,64,512]{3,0,2,1:T(4,128)} %scatter-add.4) | copy-start | bytes 12582916
